TPU v7x, 256 devices: a whole 4x4x8 slice. The times are simulated.
256 devices in a mesh: fsdp: 4 (over x), seq: 64 (over z, y, core).
Axes of the slice: x: 4, y: 4, z: 8, core: 2. Of those that a mesh axis runs over, the one named last changes fastest.
Arguments:
- tokens: bfloat16 [4, 16384, 4096], P('fsdp', 'seq'), may hold values from -6 to 6
- queries: bfloat16 [4, 16384, 4096], P('fsdp', 'seq'), may hold values from -70 to 70
- key_weight: bfloat16 [4096, 1024], P(('fsdp', 'seq')), may hold values from -0.09375 to 0.09375
- value_weight: bfloat16 [4096, 1024], P(('fsdp', 'seq')), may hold values from -0.09375 to 0.09375
- sorted_blocks: int32 [4, 8, 128], P('fsdp', None, 'seq'), may hold values from 0 to 127, as said below
Outputs:
- attended: bfloat16 [4, 16384, 4096], P('fsdp', 'seq')
Inputs may be any that keep to these rules, and one draw needn't show every extreme that they name: `sorted_blocks`: for each sequence and key-value head, a permutation of the 128 blocks. The 2 blocks of one device, over all key-value heads, name blocks that lie on one device at most 1 times, and for one head at most 1 times; both bounds are reached in every draw. Device d holds blocks d * 2 to d * 2 + 1.
All inputs are finite; a program needn't handle non-finite values.
Results may differ from a plain program's by a relative error of at most 0.012.
The roundings to bfloat16 on the way count: a program that leaves them out, or rounds other values in their place, can miss the bound.
Values may be sent and summed in bfloat16 or wider, within the bound.
A program may use at most 128 MiB of HBM per device.

v0:
```python
import math
import jax
import jax.numpy as jnp
from jax import lax
from jax.sharding import PartitionSpec as P

DH = 128
KVH = 8
GROUP = 4
BLOCK = 128


def shifted(value, axis, steps):
    count = lax.axis_size(axis)
    first, last = (max(0, -steps), min(count, count - steps))
    return lax.ppermute(value, axis, [(source, source + steps) for source in range(first, last)])


def fetch_blocks(kv_table, target_dev, target_row, devices, capacity, send_requests, send_blocks):
    item_count = target_dev.shape[0]
    item_order = jnp.arange(item_count, dtype=jnp.int32)
    same_dev = target_dev[:, None] == target_dev[None, :]
    earlier = item_order[None, :] < item_order[:, None]
    ranking = jnp.sum((same_dev & earlier).astype(jnp.int32), axis=1)
    dev_hit = target_dev[:, None, None] == jnp.arange(devices, dtype=jnp.int32)[None, :, None]
    slot_hit = ranking[:, None, None] == jnp.arange(capacity, dtype=jnp.int32)[None, None, :]
    requests = jnp.sum(jnp.where(dev_hit & slot_hit, (target_row + 1)[:, None, None], 0), axis=0)
    wanted = send_requests(requests)
    replies = jnp.take(kv_table, jnp.maximum(wanted - 1, 0), axis=0)
    replies = jnp.where((wanted > 0)[:, :, None, None], replies, jnp.zeros_like(replies))
    arrived = send_blocks(replies)
    arrived = arrived.reshape(devices * capacity, arrived.shape[2], arrived.shape[3])
    return jnp.take(arrived, target_dev * capacity + ranking, axis=0)


def local(tokens, queries, key_weight, value_weight, sorted_blocks):
    token_rows = tokens[0]
    local_tokens = token_rows.shape[0]
    local_blocks = local_tokens // BLOCK
    devices = lax.axis_size("seq")
    key_sums = jnp.dot(
        token_rows,
        lax.all_gather(key_weight, ("fsdp", "seq"), axis=0, tiled=True),
        preferred_element_type=jnp.float32,
    )
    value_sums = jnp.dot(
        token_rows,
        lax.all_gather(value_weight, ("fsdp", "seq"), axis=0, tiled=True),
        preferred_element_type=jnp.float32,
    )
    key_blocks = key_sums.astype(jnp.bfloat16).reshape(local_blocks, BLOCK, KVH, DH)
    value_blocks = value_sums.astype(jnp.bfloat16).reshape(local_blocks, BLOCK, KVH, DH)
    packed = jnp.concatenate([key_blocks, value_blocks], axis=3).transpose(2, 0, 1, 3)
    prev_edge = shifted(packed[:, local_blocks - 1], "seq", 1)
    preceding = jnp.concatenate([prev_edge[:, None], packed[:, : local_blocks - 1]], axis=1)
    targets = sorted_blocks[0]
    target_dev = targets // local_blocks
    target_slot = targets % local_blocks
    capacity = (local_blocks + devices - 1) // devices
    gathered_heads = []
    for kv_head in range(KVH):
        gathered_heads.append(
            fetch_blocks(
                packed[kv_head],
                target_dev[kv_head],
                target_slot[kv_head],
                devices,
                capacity,
                lambda payload: lax.all_to_all(
                    payload, "seq", split_axis=0, concat_axis=0, tiled=True
                ),
                lambda payload: lax.all_to_all(
                    payload, "seq", split_axis=0, concat_axis=0, tiled=True
                ),
            )
        )
    sorted_kv = jnp.stack(gathered_heads, axis=0)
    candidates = jnp.concatenate([packed, preceding, sorted_kv], axis=2)
    key_part = candidates[:, :, :, :DH]
    value_part = candidates[:, :, :, DH:]
    query_blocks = queries[0].reshape(local_blocks, BLOCK, KVH, GROUP, DH)
    scores = jnp.einsum(
        "bthge,hbke->hgbtk", query_blocks, key_part, preferred_element_type=jnp.float32
    ) * (1.0 / math.sqrt(DH))
    block_index = lax.axis_index("seq") * local_blocks + jnp.arange(local_blocks, dtype=jnp.int32)
    key_index = jnp.arange(3 * BLOCK, dtype=jnp.int32)
    blocked = (
        (block_index[:, None] == 0)
        & (key_index[None, :] >= BLOCK)
        & (key_index[None, :] < 2 * BLOCK)
    )
    scores = jnp.where(blocked[None, None, :, None, :], -1e30, scores)
    highest = jnp.max(scores, axis=-1, keepdims=True)
    raised = jnp.exp(scores - highest)
    weights = (raised / jnp.sum(raised, axis=-1, keepdims=True)).astype(jnp.bfloat16)
    result = jnp.einsum(
        "hgbtk,hbke->bthge", weights, value_part, preferred_element_type=jnp.float32
    )
    return result.astype(jnp.bfloat16).reshape(1, local_tokens, KVH * GROUP * DH)


def solution(mesh):
    placed = (
        P("fsdp", "seq", None),
        P("fsdp", "seq", None),
        P(("fsdp", "seq"), None),
        P(("fsdp", "seq"), None),
        P("fsdp", None, "seq"),
    )
    return jax.shard_map(
        local, mesh=mesh, in_specs=placed, out_specs=P("fsdp", "seq", None), check_vma=False
    )
```

profile of v0, /device:TPU:1, one launch (start us, length us, event | category | flops | bytes accessed | tf_op | source)
XLA Modules:
  0.0 1156.5 jit_solution(5378206535577151252)
XLA Ops:
  10.1 13.2 %all-to-all-start.14 = ((s32[64,1,1]{2,1,0:T(1,128)}), s32[64,1,1]{2,1,0:T(1,128)S(1)}, u32[]{:S(2)}, u32[]{:S(2)}) async-start(s32[64,1,1]{2,1,0:T(1,128)} %copy.82), calls=%async_computation.14 | async-start | bytes 65536 | tf_op jit(solution)/shard_map/all_to_all | solution.py:69
  33.3 10.3 all-to-all-start
  57.6 9.5 all-to-all-done.2
  71.7 62.1 %all-gather.3.cloned.1.call-done = bf16[4096,1024]{1,0:T(8,128)(2,1)} async-done(((bf16[16,1024]{1,0:T(8,128)(2,1)}), bf16[4096,1024]{1,0:T(8,128)(2,1)}) %all-gather.3.cloned.1.call-update) | async-done | bytes 8388624 | tf_op jit(solution)/shard_map/all_gather | solution.py:43
  139.5 6.9 all-to-all-start.6
  146.4 106.1 %all-gather.5.cloned.1.call-done = bf16[4096,1024]{1,0:T(8,128)(2,1)} async-done(((bf16[16,1024]{1,0:T(8,128)(2,1)}), bf16[4096,1024]{1,0:T(8,128)(2,1)}) %all-gather.5.cloned.1.call-update) | async-done | bytes 8388624 | tf_op jit(solution)/shard_map/all_gather | solution.py:48
  265.7 9.2 all-to-all-done.8
  318.3 85.4 %all-to-all-done.15 = bf16[64,1,128,256]{3,2,1,0:T(8,128)(2,1)} async-done(((bf16[64,1,128,256]{3,2,1,0:T(8,128)(2,1)}), bf16[64,1,128,256]{3,2,1,0:T(8,128)(2,1)}, u32[]{:S(2)}, u32[]{:S(2)}) %all-to-all-start.15) | async-done | bytes 4194336 | tf_op jit(solution)/shard_map/all_to_all | solution.py:72
  403.7 7.2 all-to-all-start.11
  420.1 85.4 %all-to-all-done.11 = bf16[64,1,128,256]{3,2,1,0:T(8,128)(2,1)} async-done(((bf16[64,1,128,256]{3,2,1,0:T(8,128)(2,1)}), bf16[64,1,128,256]{3,2,1,0:T(8,128)(2,1)}, u32[]{:S(2)}, u32[]{:S(2)}) %all-to-all-start.11) | async-done | bytes 4194336 | tf_op jit(solution)/shard_map/all_to_all | solution.py:72
  505.6 7.6 all-to-all-start.9
  522.4 85.2 %all-to-all-done.9 = bf16[64,1,128,256]{3,2,1,0:T(8,128)(2,1)} async-done(((bf16[64,1,128,256]{3,2,1,0:T(8,128)(2,1)}), bf16[64,1,128,256]{3,2,1,0:T(8,128)(2,1)}, u32[]{:S(2)}, u32[]{:S(2)}) %all-to-all-start.9) | async-done | bytes 4194336 | tf_op jit(solution)/shard_map/all_to_all | solution.py:72
  607.6 7.2 all-to-all-start.7
  624.0 85.5 %all-to-all-done.7 = bf16[64,1,128,256]{3,2,1,0:T(8,128)(2,1)} async-done(((bf16[64,1,128,256]{3,2,1,0:T(8,128)(2,1)}), bf16[64,1,128,256]{3,2,1,0:T(8,128)(2,1)}, u32[]{:S(2)}, u32[]{:S(2)}) %all-to-all-start.7) | async-done | bytes 4194336 | tf_op jit(solution)/shard_map/all_to_all | solution.py:72
  709.5 7.2 all-to-all-start.5
  726.0 85.5 %all-to-all-done.5 = bf16[64,1,128,256]{3,2,1,0:T(8,128)(2,1)} async-done(((bf16[64,1,128,256]{3,2,1,0:T(8,128)(2,1)}), bf16[64,1,128,256]{3,2,1,0:T(8,128)(2,1)}, u32[]{:S(2)}, u32[]{:S(2)}) %all-to-all-start.5) | async-done | bytes 4194336 | tf_op jit(solution)/shard_map/all_to_all | solution.py:72
  811.5 7.6 all-to-all-start.3
  828.3 85.3 %all-to-all-done.3 = bf16[64,1,128,256]{3,2,1,0:T(8,128)(2,1)} async-done(((bf16[64,1,128,256]{3,2,1,0:T(8,128)(2,1)}), bf16[64,1,128,256]{3,2,1,0:T(8,128)(2,1)}, u32[]{:S(2)}, u32[]{:S(2)}) %all-to-all-start.3) | async-done | bytes 4194336 | tf_op jit(solution)/shard_map/all_to_all | solution.py:72
  913.6 7.2 all-to-all-start.1
  930.2 85.3 %all-to-all-done.1 = bf16[64,1,128,256]{3,2,1,0:T(8,128)(2,1)} async-done(((bf16[64,1,128,256]{3,2,1,0:T(8,128)(2,1)}), bf16[64,1,128,256]{3,2,1,0:T(8,128)(2,1)}, u32[]{:S(2)}, u32[]{:S(2)}) %all-to-all-start.1) | async-done | bytes 4194336 | tf_op jit(solution)/shard_map/all_to_all | solution.py:72
  1015.5 7.2 all-to-all-start.13
  1058.8 59.7 %all-to-all-done.13 = bf16[64,1,128,256]{3,2,1,0:T(8,128)(2,1)} async-done(((bf16[64,1,128,256]{3,2,1,0:T(8,128)(2,1)}), bf16[64,1,128,256]{3,2,1,0:T(8,128)(2,1)}, u32[]{:S(2)}, u32[]{:S(2)}) %all-to-all-start.13) | async-done | bytes 4194336 | tf_op jit(solution)/shard_map/all_to_all | solution.py:72
  1123.3 9.2 fusion.80
  1132.5 7.9 convert_bitcast_fusion
  (152 shorter events, 199.3 us)
Async XLA Ops:
  6.5 127.2 %copy-start = (bf16[1,256,4096]{2,1,0:T(8,128)(2,1)S(1)}, bf16[1,256,4096]{2,1,0:T(8,128)(2,1)}, u32[]{:S(2)}) copy-start(bf16[1,256,4096]{2,1,0:T(8,128)(2,1)} %param.9) | copy-start | bytes 6291460
  6.5 127.2 %all-gather.3.cloned.1.call-start = ((), (), s32[]{:S(2)}) async-start(), calls=%async_computation.16 | async-start | bytes 8421376 | tf_op jit(solution)/shard_map/all_gather | solution.py:43
  7.3 245.3 %all-gather.5.cloned.1.call-start = ((), (), s32[]{:S(2)}) async-start(), calls=%async_computation.17 | async-start | bytes 8421376 | tf_op jit(solution)/shard_map/all_gather | solution.py:48
  10.1 23.2 %all-to-all-start.14 = ((s32[64,1,1]{2,1,0:T(1,128)}), s32[64,1,1]{2,1,0:T(1,128)S(1)}, u32[]{:S(2)}, u32[]{:S(2)}) async-start(s32[64,1,1]{2,1,0:T(1,128)} %copy.82), calls=%async_computation.14 | async-start | bytes 65536 | tf_op jit(solution)/shard_map/all_to_all | solution.py:69
  33.3 19.6 %all-to-all-start = ((s32[64,1,1]{2,1,0:T(1,128)}), s32[64,1,1]{2,1,0:T(1,128)S(1)}, u32[]{:S(2)}, u32[]{:S(2)}) async-start(s32[64,1,1]{2,1,0:T(1,128)} %copy.68), calls=%async_computation | async-start | bytes 65536 | tf_op jit(solution)/shard_map/all_to_all | solution.py:69
  52.9 14.1 %all-to-all-start.2 = ((s32[64,1,1]{2,1,0:T(1,128)}), s32[64,1,1]{2,1,0:T(1,128)S(1)}, u32[]{:S(2)}, u32[]{:S(2)}) async-start(s32[64,1,1]{2,1,0:T(1,128)} %copy.70), calls=%async_computation.2 | async-start | bytes 65536 | tf_op jit(solution)/shard_map/all_to_all | solution.py:69
  67.1 72.4 %all-to-all-start.4 = ((s32[64,1,1]{2,1,0:T(1,128)}), s32[64,1,1]{2,1,0:T(1,128)S(1)}, u32[]{:S(2)}, u32[]{:S(2)}) async-start(s32[64,1,1]{2,1,0:T(1,128)} %copy.72), calls=%async_computation.4 | async-start | bytes 65536 | tf_op jit(solution)/shard_map/all_to_all | solution.py:69
  139.5 119.2 %all-to-all-start.6 = ((s32[64,1,1]{2,1,0:T(1,128)}), s32[64,1,1]{2,1,0:T(1,128)S(1)}, u32[]{:S(2)}, u32[]{:S(2)}) async-start(s32[64,1,1]{2,1,0:T(1,128)} %copy.74), calls=%async_computation.6 | async-start | bytes 65536 | tf_op jit(solution)/shard_map/all_to_all | solution.py:69
  258.7 16.3 %all-to-all-start.8 = ((s32[64,1,1]{2,1,0:T(1,128)}), s32[64,1,1]{2,1,0:T(1,128)S(1)}, u32[]{:S(2)}, u32[]{:S(2)}) async-start(s32[64,1,1]{2,1,0:T(1,128)} %copy.76), calls=%async_computation.8 | async-start | bytes 65536 | tf_op jit(solution)/shard_map/all_to_all | solution.py:69
  275.0 14.2 %all-to-all-start.10 = ((s32[64,1,1]{2,1,0:T(1,128)}), s32[64,1,1]{2,1,0:T(1,128)S(1)}, u32[]{:S(2)}, u32[]{:S(2)}) async-start(s32[64,1,1]{2,1,0:T(1,128)} %copy.78), calls=%async_computation.10 | async-start | bytes 65536 | tf_op jit(solution)/shard_map/all_to_all | solution.py:69
  289.2 14.1 %all-to-all-start.12 = ((s32[64,1,1]{2,1,0:T(1,128)}), s32[64,1,1]{2,1,0:T(1,128)S(1)}, u32[]{:S(2)}, u32[]{:S(2)}) async-start(s32[64,1,1]{2,1,0:T(1,128)} %copy.80), calls=%async_computation.12 | async-start | bytes 65536 | tf_op jit(solution)/shard_map/all_to_all | solution.py:69
  303.3 100.3 %all-to-all-start.15 = ((bf16[64,1,128,256]{3,2,1,0:T(8,128)(2,1)}), bf16[64,1,128,256]{3,2,1,0:T(8,128)(2,1)}, u32[]{:S(2)}, u32[]{:S(2)}) async-start(bf16[64,1,128,256]{3,2,1,0:T(8,128)(2,1)} %fusion.13), calls=%async_computation.15 | async-start | bytes 8388608 | tf_op jit(solution)/shard_map/all_to_all | solution.py:72
  403.7 101.9 %all-to-all-start.11 = ((bf16[64,1,128,256]{3,2,1,0:T(8,128)(2,1)}), bf16[64,1,128,256]{3,2,1,0:T(8,128)(2,1)}, u32[]{:S(2)}, u32[]{:S(2)}) async-start(bf16[64,1,128,256]{3,2,1,0:T(8,128)(2,1)} %fusion.17), calls=%async_computation.11 | async-start | bytes 8388608 | tf_op jit(solution)/shard_map/all_to_all | solution.py:72
  505.6 102.1 %all-to-all-start.9 = ((bf16[64,1,128,256]{3,2,1,0:T(8,128)(2,1)}), bf16[64,1,128,256]{3,2,1,0:T(8,128)(2,1)}, u32[]{:S(2)}, u32[]{:S(2)}) async-start(bf16[64,1,128,256]{3,2,1,0:T(8,128)(2,1)} %fusion.19), calls=%async_computation.9 | async-start | bytes 8388608 | tf_op jit(solution)/shard_map/all_to_all | solution.py:72
  607.6 101.9 %all-to-all-start.7 = ((bf16[64,1,128,256]{3,2,1,0:T(8,128)(2,1)}), bf16[64,1,128,256]{3,2,1,0:T(8,128)(2,1)}, u32[]{:S(2)}, u32[]{:S(2)}) async-start(bf16[64,1,128,256]{3,2,1,0:T(8,128)(2,1)} %fusion.21), calls=%async_computation.7 | async-start | bytes 8388608 | tf_op jit(solution)/shard_map/all_to_all | solution.py:72
  709.5 101.9 %all-to-all-start.5 = ((bf16[64,1,128,256]{3,2,1,0:T(8,128)(2,1)}), bf16[64,1,128,256]{3,2,1,0:T(8,128)(2,1)}, u32[]{:S(2)}, u32[]{:S(2)}) async-start(bf16[64,1,128,256]{3,2,1,0:T(8,128)(2,1)} %fusion.23), calls=%async_computation.5 | async-start | bytes 8388608 | tf_op jit(solution)/shard_map/all_to_all | solution.py:72
  811.5 102.1 %all-to-all-start.3 = ((bf16[64,1,128,256]{3,2,1,0:T(8,128)(2,1)}), bf16[64,1,128,256]{3,2,1,0:T(8,128)(2,1)}, u32[]{:S(2)}, u32[]{:S(2)}) async-start(bf16[64,1,128,256]{3,2,1,0:T(8,128)(2,1)} %fusion.25), calls=%async_computation.3 | async-start | bytes 8388608 | tf_op jit(solution)/shard_map/all_to_all | solution.py:72
  913.6 101.9 %all-to-all-start.1 = ((bf16[64,1,128,256]{3,2,1,0:T(8,128)(2,1)}), bf16[64,1,128,256]{3,2,1,0:T(8,128)(2,1)}, u32[]{:S(2)}, u32[]{:S(2)}) async-start(bf16[64,1,128,256]{3,2,1,0:T(8,128)(2,1)} %fusion.27), calls=%async_computation.1 | async-start | bytes 8388608 | tf_op jit(solution)/shard_map/all_to_all | solution.py:72
  1015.5 103.1 %all-to-all-start.13 = ((bf16[64,1,128,256]{3,2,1,0:T(8,128)(2,1)}), bf16[64,1,128,256]{3,2,1,0:T(8,128)(2,1)}, u32[]{:S(2)}, u32[]{:S(2)}) async-start(bf16[64,1,128,256]{3,2,1,0:T(8,128)(2,1)} %fusion.15), calls=%async_computation.13 | async-start | bytes 8388608 | tf_op jit(solution)/shard_map/all_to_all | solution.py:72
  1028.8 92.6 %collective-permute-start = (bf16[8,128,256]{2,1,0:T(8,128)(2,1)}, bf16[8,128,256]{2,1,0:T(8,128)(2,1)S(1)}, u32[]{:S(2)}, u32[]{:S(2)}) collective-permute-start(bf16[8,128,256]{2,1,0:T(8,128)(2,1)} %get-tuple-element.39), channel_id=1, source_target_pairs={{0,1},{1,2},{2,3},{3,4},{4,5},{5,6},{6,7},{7,8},{8,9},{9,10},{10,1... | collective-permute-start | bytes 1572872 | tf_op jit(solution)/shard_map/ppermute | solution.py:16
  1132.5 16.9 %copy-start.1 = (bf16[1,256,4096]{2,1,0:T(8,128)(2,1)S(1)}, bf16[1,256,4096]{2,1,0:T(8,128)(2,1)}, u32[]{:S(2)}) copy-start(bf16[1,256,4096]{2,1,0:T(8,128)(2,1)} %param.9) | copy-start | bytes 6291460
Sparse Core Ops, SparseCore 0:
  11.1 122.6 all-gather.2
  137.5 115.0 all-gather.4
where the time goes:
time: 1170 us; the launch traced here: 1160 us
  waiting for transfers between devices  864 us (74%)
  starting transfers between devices  117 us (10%)
  local copies, waits for them, and re-layouts  66.5 us (6%)
  other arithmetic  66 us (6%)
  matrix products  28.5 us (2%)
  between operations  14.2 us (1%)
    all_to_all x16, waiting for transfers between devices, local(): lax.all_to_all(payload, 'seq', split_axis=0, concat_axis=0, tiled=True)  695 us
    all_to_all x16, starting transfers between devices, local(): lax.all_to_all(payload, 'seq', split_axis=0, concat_axis=0, tiled=True)  113 us
    all_gather x1, waiting for transfers between devices, local(): lax.all_gather(value_weight, ('fsdp', 'seq'), axis=0, tiled=True)  106 us
    all_gather x1, waiting for transfers between devices, local(): lax.all_gather(key_weight, ('fsdp', 'seq'), axis=0, tiled=True)  62.1 us
    select_n x8, other arithmetic, fetch_blocks(): jnp.where((wanted > 0)[:, :, None, None], replies, jnp.zeros_like(replies))  31.8 us
    gather x8, local copies, waits for them, and re-layouts, fetch_blocks(): return jnp.take(arrived, target_dev * capacity + ranking, axis=0)  23.9 us
  transfers between devices with their start and end apart: 19, of which 15 were waited for; matrix products, arithmetic and copies ran while one was open for 12% of the time, Pallas kernels for 0%

commit v1 on v0

--- a/solution.py
+++ b/solution.py
@@ -45,7 +45,12 @@
     )
     value_sums = jnp.dot(
         token_rows,
-        lax.all_gather(value_weight, ("fsdp", "seq"), axis=0, tiled=True),
+        jnp.concatenate(
+            lax.all_to_all(
+                jnp.stack([value_weight] * lax.axis_size(("fsdp", "seq"))), ("fsdp", "seq"), 0, 0
+            ),
+            axis=0,
+        ),
         preferred_element_type=jnp.float32,
     )
     key_blocks = key_sums.astype(jnp.bfloat16).reshape(local_blocks, BLOCK, KVH, DH)

time: 1170 us -> 1220 us (1.043)
  waiting for transfers between devices: 864 us -> 897 us
  blocking collectives: 0 us -> 13.4 us
    all_to_all x0 -> x1, waiting for transfers between devices: none -> 195 us  [local(): lax.all_to_all(jnp.stack([value_weight] * lax.axis_size(('fsdp', 'seq')))...]
    all_gather x1 -> x0, waiting for transfers between devices: 106 us -> none  [local(): lax.all_gather(value_weight, ('fsdp', 'seq'), axis=0, tiled=True)]
    all_gather x1, waiting for transfers between devices: 62.1 us -> 0.02 us  [local(): lax.all_gather(key_weight, ('fsdp', 'seq'), axis=0, tiled=True)]
    all_to_all x0 -> x1, blocking collectives: none -> 13.4 us  [local(): lax.all_to_all(payload, 'seq', split_axis=0, concat_axis=0, tiled=True)]
    all_to_all x16 -> x15, starting transfers between devices: 113 us -> 104 us  [local(): lax.all_to_all(payload, 'seq', split_axis=0, concat_axis=0, tiled=True)]
    all_to_all x16 -> x15, waiting for transfers between devices: 695 us -> 702 us  [local(): lax.all_to_all(payload, 'seq', split_axis=0, concat_axis=0, tiled=True)]
  transfers between devices with their start and end apart: 19 -> 18, of which waited for: 15 -> 16; matrix products, arithmetic and copies ran while one was open for 12% -> 11% of each run, Pallas kernels for 0% -> 0%
where the time goes in v1:
time: 1220 us; the launch traced here: 1210 us
  waiting for transfers between devices  897 us (74%)
  starting transfers between devices  115 us (9%)
  local copies, waits for them, and re-layouts  71.1 us (6%)
  other arithmetic  67.6 us (6%)
  matrix products  28.5 us (2%)
  between operations  14.1 us (1%)
  blocking collectives  13.4 us (1%)
    all_to_all x15, waiting for transfers between devices, local(): lax.all_to_all(payload, 'seq', split_axis=0, concat_axis=0, tiled=True)  702 us
    all_to_all x1, waiting for transfers between devices, local(): lax.all_to_all(jnp.stack([value_weight] * lax.axis_size(('fsdp', 'seq')))...  195 us
    all_to_all x15, starting transfers between devices, local(): lax.all_to_all(payload, 'seq', split_axis=0, concat_axis=0, tiled=True)  104 us
    select_n x8, other arithmetic, fetch_blocks(): jnp.where((wanted > 0)[:, :, None, None], replies, jnp.zeros_like(replies))  31.9 us
  transfers between devices with their start and end apart: 18, of which 16 were waited for; matrix products, arithmetic and copies ran while one was open for 11% of the time, Pallas kernels for 0%

profile of v1, /device:TPU:1, one launch (start us, length us, event | category | flops | bytes accessed | tf_op | source)
XLA Modules:
  0.0 1207.3 jit_solution(10984194361841357628)
XLA Ops:
  8.8 13.2 %all-to-all-start.1 = ((s32[64,1,1]{2,1,0:T(1,128)}), s32[64,1,1]{2,1,0:T(1,128)S(1)}, u32[]{:S(2)}, u32[]{:S(2)}) async-start(s32[64,1,1]{2,1,0:T(1,128)} %copy.68), calls=%async_computation.1 | async-start | bytes 65536 | tf_op jit(solution)/shard_map/all_to_all | solution.py:74
  23.8 7.5 all-to-all-done.1
  36.1 9.3 all-to-all-done.3
  45.4 13.4 %all_to_all.117 = s32[64,1,1]{2,1,0:T(1,128)S(1)} all-to-all(s32[64,1,1]{2,1,0:T(1,128)S(1)} %copy.72), channel_id=1, replica_groups=mesh['fsdp'=4,'seq'=64] {'seq'}, dimensions={0} | all-to-all | bytes 512 | tf_op jit(solution)/shard_map/all_to_all | solution.py:74
  63.9 7.4 all-to-all-start
  82.1 194.5 %all-to-all-done = bf16[256,16,1024]{2,1,0:T(8,128)(2,1)} async-done(((bf16[256,16,1024]{2,1,0:T(8,128)(2,1)}), bf16[256,16,1024]{2,1,0:T(8,128)(2,1)}, u32[]{:S(2)}, u32[]{:S(2)}) %all-to-all-start) | async-done | bytes 8388640 | tf_op jit(solution)/shard_map/all_to_all | solution.py:49
  315.2 9.2 all-to-all-done.11
  367.7 85.4 %all-to-all-done.2 = bf16[64,1,128,256]{3,2,1,0:T(8,128)(2,1)} async-done(((bf16[64,1,128,256]{3,2,1,0:T(8,128)(2,1)}), bf16[64,1,128,256]{3,2,1,0:T(8,128)(2,1)}, u32[]{:S(2)}, u32[]{:S(2)}) %all-to-all-start.2) | async-done | bytes 4194336 | tf_op jit(solution)/shard_map/all_to_all | solution.py:77
  453.1 7.6 all-to-all-start.4
  470.0 85.2 %all-to-all-done.4 = bf16[64,1,128,256]{3,2,1,0:T(8,128)(2,1)} async-done(((bf16[64,1,128,256]{3,2,1,0:T(8,128)(2,1)}), bf16[64,1,128,256]{3,2,1,0:T(8,128)(2,1)}, u32[]{:S(2)}, u32[]{:S(2)}) %all-to-all-start.4) | async-done | bytes 4194336 | tf_op jit(solution)/shard_map/all_to_all | solution.py:77
  555.2 7.2 all-to-all-start.6
  571.6 85.5 %all-to-all-done.6 = bf16[64,1,128,256]{3,2,1,0:T(8,128)(2,1)} async-done(((bf16[64,1,128,256]{3,2,1,0:T(8,128)(2,1)}), bf16[64,1,128,256]{3,2,1,0:T(8,128)(2,1)}, u32[]{:S(2)}, u32[]{:S(2)}) %all-to-all-start.6) | async-done | bytes 4194336 | tf_op jit(solution)/shard_map/all_to_all | solution.py:77
  657.1 7.2 all-to-all-start.8
  673.6 85.4 %all-to-all-done.8 = bf16[64,1,128,256]{3,2,1,0:T(8,128)(2,1)} async-done(((bf16[64,1,128,256]{3,2,1,0:T(8,128)(2,1)}), bf16[64,1,128,256]{3,2,1,0:T(8,128)(2,1)}, u32[]{:S(2)}, u32[]{:S(2)}) %all-to-all-start.8) | async-done | bytes 4194336 | tf_op jit(solution)/shard_map/all_to_all | solution.py:77
  759.0 7.8 all-to-all-start.10
  776.1 85.2 %all-to-all-done.10 = bf16[64,1,128,256]{3,2,1,0:T(8,128)(2,1)} async-done(((bf16[64,1,128,256]{3,2,1,0:T(8,128)(2,1)}), bf16[64,1,128,256]{3,2,1,0:T(8,128)(2,1)}, u32[]{:S(2)}, u32[]{:S(2)}) %all-to-all-start.10) | async-done | bytes 4194336 | tf_op jit(solution)/shard_map/all_to_all | solution.py:77
  861.3 7.2 all-to-all-start.12
  878.0 85.2 %all-to-all-done.12 = bf16[64,1,128,256]{3,2,1,0:T(8,128)(2,1)} async-done(((bf16[64,1,128,256]{3,2,1,0:T(8,128)(2,1)}), bf16[64,1,128,256]{3,2,1,0:T(8,128)(2,1)}, u32[]{:S(2)}, u32[]{:S(2)}) %all-to-all-start.12) | async-done | bytes 4194336 | tf_op jit(solution)/shard_map/all_to_all | solution.py:77
  963.2 7.2 all-to-all-start.14
  979.7 85.4 %all-to-all-done.14 = bf16[64,1,128,256]{3,2,1,0:T(8,128)(2,1)} async-done(((bf16[64,1,128,256]{3,2,1,0:T(8,128)(2,1)}), bf16[64,1,128,256]{3,2,1,0:T(8,128)(2,1)}, u32[]{:S(2)}, u32[]{:S(2)}) %all-to-all-start.14) | async-done | bytes 4194336 | tf_op jit(solution)/shard_map/all_to_all | solution.py:77
  1065.1 7.2 all-to-all-start.16
  1108.5 59.7 %all-to-all-done.16 = bf16[64,1,128,256]{3,2,1,0:T(8,128)(2,1)} async-done(((bf16[64,1,128,256]{3,2,1,0:T(8,128)(2,1)}), bf16[64,1,128,256]{3,2,1,0:T(8,128)(2,1)}, u32[]{:S(2)}, u32[]{:S(2)}) %all-to-all-start.16) | async-done | bytes 4194336 | tf_op jit(solution)/shard_map/all_to_all | solution.py:77
  1174.1 9.2 fusion.80
  1183.3 7.9 convert_bitcast_fusion
  (153 shorter events, 212.9 us)
Async XLA Ops:
  6.5 275.7 %copy-start = (bf16[1,256,4096]{2,1,0:T(8,128)(2,1)S(1)}, bf16[1,256,4096]{2,1,0:T(8,128)(2,1)}, u32[]{:S(2)}) copy-start(bf16[1,256,4096]{2,1,0:T(8,128)(2,1)} %param.9) | copy-start | bytes 6291460
  8.8 22.5 %all-to-all-start.1 = ((s32[64,1,1]{2,1,0:T(1,128)}), s32[64,1,1]{2,1,0:T(1,128)S(1)}, u32[]{:S(2)}, u32[]{:S(2)}) async-start(s32[64,1,1]{2,1,0:T(1,128)} %copy.68), calls=%async_computation.1 | async-start | bytes 65536 | tf_op jit(solution)/shard_map/all_to_all | solution.py:74
  31.3 14.1 %all-to-all-start.3 = ((s32[64,1,1]{2,1,0:T(1,128)}), s32[64,1,1]{2,1,0:T(1,128)S(1)}, u32[]{:S(2)}, u32[]{:S(2)}) async-start(s32[64,1,1]{2,1,0:T(1,128)} %copy.70), calls=%async_computation.3 | async-start | bytes 65536 | tf_op jit(solution)/shard_map/all_to_all | solution.py:74
  63.9 212.8 %all-to-all-start = ((bf16[256,16,1024]{2,1,0:T(8,128)(2,1)}), bf16[256,16,1024]{2,1,0:T(8,128)(2,1)}, u32[]{:S(2)}, u32[]{:S(2)}) async-start(bf16[256,16,1024]{2,1,0:T(8,128)(2,1)} %stack.20), calls=%async_computation | async-start | bytes 16777216 | tf_op jit(solution)/shard_map/all_to_all | solution.py:49
  71.3 227.3 %all-gather.2.cloned.1.call-start = ((), (), s32[]{:S(2)}) async-start(), calls=%async_computation.17 | async-start | bytes 8421376 | tf_op jit(solution)/shard_map/all_gather | solution.py:43
  276.7 14.9 %all-to-all-start.7 = ((s32[64,1,1]{2,1,0:T(1,128)}), s32[64,1,1]{2,1,0:T(1,128)S(1)}, u32[]{:S(2)}, u32[]{:S(2)}) async-start(s32[64,1,1]{2,1,0:T(1,128)} %copy.74), calls=%async_computation.7 | async-start | bytes 65536 | tf_op jit(solution)/shard_map/all_to_all | solution.py:74
  291.5 16.4 %all-to-all-start.9 = ((s32[64,1,1]{2,1,0:T(1,128)}), s32[64,1,1]{2,1,0:T(1,128)S(1)}, u32[]{:S(2)}, u32[]{:S(2)}) async-start(s32[64,1,1]{2,1,0:T(1,128)} %copy.76), calls=%async_computation.9 | async-start | bytes 65536 | tf_op jit(solution)/shard_map/all_to_all | solution.py:74
  307.9 16.5 %all-to-all-start.11 = ((s32[64,1,1]{2,1,0:T(1,128)}), s32[64,1,1]{2,1,0:T(1,128)S(1)}, u32[]{:S(2)}, u32[]{:S(2)}) async-start(s32[64,1,1]{2,1,0:T(1,128)} %copy.78), calls=%async_computation.11 | async-start | bytes 65536 | tf_op jit(solution)/shard_map/all_to_all | solution.py:74
  324.4 14.2 %all-to-all-start.13 = ((s32[64,1,1]{2,1,0:T(1,128)}), s32[64,1,1]{2,1,0:T(1,128)S(1)}, u32[]{:S(2)}, u32[]{:S(2)}) async-start(s32[64,1,1]{2,1,0:T(1,128)} %copy.80), calls=%async_computation.13 | async-start | bytes 65536 | tf_op jit(solution)/shard_map/all_to_all | solution.py:74
  338.6 14.2 %all-to-all-start.15 = ((s32[64,1,1]{2,1,0:T(1,128)}), s32[64,1,1]{2,1,0:T(1,128)S(1)}, u32[]{:S(2)}, u32[]{:S(2)}) async-start(s32[64,1,1]{2,1,0:T(1,128)} %copy.82), calls=%async_computation.15 | async-start | bytes 65536 | tf_op jit(solution)/shard_map/all_to_all | solution.py:74
  352.8 100.4 %all-to-all-start.2 = ((bf16[64,1,128,256]{3,2,1,0:T(8,128)(2,1)}), bf16[64,1,128,256]{3,2,1,0:T(8,128)(2,1)}, u32[]{:S(2)}, u32[]{:S(2)}) async-start(bf16[64,1,128,256]{3,2,1,0:T(8,128)(2,1)} %fusion.27), calls=%async_computation.2 | async-start | bytes 8388608 | tf_op jit(solution)/shard_map/all_to_all | solution.py:77
  453.1 102.1 %all-to-all-start.4 = ((bf16[64,1,128,256]{3,2,1,0:T(8,128)(2,1)}), bf16[64,1,128,256]{3,2,1,0:T(8,128)(2,1)}, u32[]{:S(2)}, u32[]{:S(2)}) async-start(bf16[64,1,128,256]{3,2,1,0:T(8,128)(2,1)} %fusion.25), calls=%async_computation.4 | async-start | bytes 8388608 | tf_op jit(solution)/shard_map/all_to_all | solution.py:77
  555.2 101.9 %all-to-all-start.6 = ((bf16[64,1,128,256]{3,2,1,0:T(8,128)(2,1)}), bf16[64,1,128,256]{3,2,1,0:T(8,128)(2,1)}, u32[]{:S(2)}, u32[]{:S(2)}) async-start(bf16[64,1,128,256]{3,2,1,0:T(8,128)(2,1)} %fusion.23), calls=%async_computation.6 | async-start | bytes 8388608 | tf_op jit(solution)/shard_map/all_to_all | solution.py:77
  657.1 101.9 %all-to-all-start.8 = ((bf16[64,1,128,256]{3,2,1,0:T(8,128)(2,1)}), bf16[64,1,128,256]{3,2,1,0:T(8,128)(2,1)}, u32[]{:S(2)}, u32[]{:S(2)}) async-start(bf16[64,1,128,256]{3,2,1,0:T(8,128)(2,1)} %fusion.21), calls=%async_computation.8 | async-start | bytes 8388608 | tf_op jit(solution)/shard_map/all_to_all | solution.py:77
  759.0 102.3 %all-to-all-start.10 = ((bf16[64,1,128,256]{3,2,1,0:T(8,128)(2,1)}), bf16[64,1,128,256]{3,2,1,0:T(8,128)(2,1)}, u32[]{:S(2)}, u32[]{:S(2)}) async-start(bf16[64,1,128,256]{3,2,1,0:T(8,128)(2,1)} %fusion.19), calls=%async_computation.10 | async-start | bytes 8388608 | tf_op jit(solution)/shard_map/all_to_all | solution.py:77
  861.3 101.9 %all-to-all-start.12 = ((bf16[64,1,128,256]{3,2,1,0:T(8,128)(2,1)}), bf16[64,1,128,256]{3,2,1,0:T(8,128)(2,1)}, u32[]{:S(2)}, u32[]{:S(2)}) async-start(bf16[64,1,128,256]{3,2,1,0:T(8,128)(2,1)} %fusion.17), calls=%async_computation.12 | async-start | bytes 8388608 | tf_op jit(solution)/shard_map/all_to_all | solution.py:77
  963.2 101.9 %all-to-all-start.14 = ((bf16[64,1,128,256]{3,2,1,0:T(8,128)(2,1)}), bf16[64,1,128,256]{3,2,1,0:T(8,128)(2,1)}, u32[]{:S(2)}, u32[]{:S(2)}) async-start(bf16[64,1,128,256]{3,2,1,0:T(8,128)(2,1)} %fusion.15), calls=%async_computation.14 | async-start | bytes 8388608 | tf_op jit(solution)/shard_map/all_to_all | solution.py:77
  1065.1 103.1 %all-to-all-start.16 = ((bf16[64,1,128,256]{3,2,1,0:T(8,128)(2,1)}), bf16[64,1,128,256]{3,2,1,0:T(8,128)(2,1)}, u32[]{:S(2)}, u32[]{:S(2)}) async-start(bf16[64,1,128,256]{3,2,1,0:T(8,128)(2,1)} %fusion.13), calls=%async_computation.16 | async-start | bytes 8388608 | tf_op jit(solution)/shard_map/all_to_all | solution.py:77
  1078.5 93.9 %collective-permute-start = (bf16[8,128,256]{2,1,0:T(8,128)(2,1)}, bf16[8,128,256]{2,1,0:T(8,128)(2,1)S(1)}, u32[]{:S(2)}, u32[]{:S(2)}) collective-permute-start(bf16[8,128,256]{2,1,0:T(8,128)(2,1)} %get-tuple-element.39), channel_id=1, source_target_pairs={{0,1},{1,2},{2,3},{3,4},{4,5},{5,6},{6,7},{7,8},{8,9},{9,10},{10,1... | collective-permute-start | bytes 1572872 | tf_op jit(solution)/shard_map/ppermute | solution.py:16
  1102.6 71.6 %copy-start.2 = (pred[2,384]{1,0:T(4,128)(4,1)S(1)}, pred[2,384]{1,0:T(4,128)(4,1)}, u32[]{:S(2)}) copy-start(pred[2,384]{1,0:T(4,128)(4,1)} %and_and_fusion) | copy-start | bytes 2308
  1183.3 16.9 %copy-start.1 = (bf16[1,256,4096]{2,1,0:T(8,128)(2,1)S(1)}, bf16[1,256,4096]{2,1,0:T(8,128)(2,1)}, u32[]{:S(2)}) copy-start(bf16[1,256,4096]{2,1,0:T(8,128)(2,1)} %param.9) | copy-start | bytes 6291460
Sparse Core Ops, SparseCore 0:
  75.8 165.3 all-gather.1
